TPU v7x, 32 devices: a whole 2x2x4 slice. The times are simulated.
32 devices in a mesh: col: 4 (over y, x), bulk: 8 (over z, core).
Axes of the slice: x: 2, y: 2, z: 4, core: 2. Of those that a mesh axis runs over, the one named last changes fastest.
Arguments:
- sequence_embedding: bfloat16 [64, 128, 64], P('bulk', 'col'), may hold values from -6 to 6
- residue_couplings: bfloat16 [128, 128, 128], P('bulk', 'col'), may hold values from -6 to 6
- sequence_layernorm_factor: float32 [64], replicated, may hold values from 0.5 to 1.5
- coupling_layernorm_factor: float32 [128], replicated, may hold values from 0.5 to 1.5
- content_projection: bfloat16 [64, 256], replicated, may hold values from -0.75 to 0.75
- switch_projection: bfloat16 [64, 256], replicated, may hold values from -0.75 to 0.75
- attention_score_projection: bfloat16 [128, 8], replicated, may hold values from -0.29882812 to 0.29882812
- final_projection: bfloat16 [256, 64], replicated, may hold values from -2 to 2
- residual_change_cotangent: bfloat16 [64, 128, 64], P('bulk', 'col'), may hold values from -6 to 6
Outputs:
- residual_change: bfloat16 [64, 128, 64], P('bulk', 'col')
- sequence_embedding_sensitivity: bfloat16 [64, 128, 64], P('bulk', 'col')
- coupling_sensitivity: bfloat16 [128, 128, 128], P('bulk', 'col')
All inputs are finite; a program needn't handle non-finite values.
Results may differ from a plain program's by a relative error of at most 0.025.
Values may be sent and summed in bfloat16 or wider, within the bound.
A program may use at most 64 MiB of HBM per device.

v0:
```python
import jax
import jax.numpy as jnp
from jax import lax
from jax.sharding import PartitionSpec as P

epsilon = 1e-05


def centred_sequences(inputs, scale_gain):
    widened = inputs.astype(jnp.float32)
    row_mean = jnp.mean(widened, axis=-1, keepdims=True)
    centered = widened - row_mean
    variance = jnp.mean(centered * centered, axis=-1, keepdims=True)
    inv_std = lax.rsqrt(variance + epsilon)
    normed = centered * inv_std
    return (normed * scale_gain, normed, inv_std)


def layernorm_reverse_mode(upstream, normed, inv_std, scale_gain):
    scaled = upstream * scale_gain
    mean_grad = jnp.mean(scaled, axis=-1, keepdims=True)
    mean_proj = jnp.mean(scaled * normed, axis=-1, keepdims=True)
    return inv_std * (scaled - mean_grad - normed * mean_proj)


def per_device(
    sequence_embedding,
    residue_couplings,
    sequence_layernorm_factor,
    coupling_layernorm_factor,
    content_projection,
    switch_projection,
    attention_score_projection,
    final_projection,
    residual_change_cotangent,
):
    number_of_heads = attention_score_projection.shape[1]
    value_channels = content_projection.shape[1]
    head_channels = value_channels // number_of_heads
    device_sequences = sequence_embedding.shape[0]
    device_residues = sequence_embedding.shape[1]
    finest_accuracy = lax.Precision.HIGHEST
    out_wide = final_projection.astype(jnp.float32)
    switch_single_form = switch_projection.astype(jnp.float32)
    bias_wide = attention_score_projection.astype(jnp.float32)
    pair_scaled, pair_hat, pair_inv = centred_sequences(
        residue_couplings, coupling_layernorm_factor
    )
    logits = jnp.einsum(
        "ijk,kh->hij",
        pair_scaled.astype(jnp.bfloat16),
        attention_score_projection,
        preferred_element_type=jnp.float32,
    )
    exponent = jnp.exp(logits)
    totals = lax.psum(jnp.sum(exponent, axis=2), "col")
    weights = exponent / totals[:, :, None]
    weights_low = weights.astype(jnp.bfloat16)
    weight_panel = lax.all_gather(weights_low, "bulk", axis=1, tiled=True)
    all_tokens = weight_panel.shape[1]
    sequence_scaled_by_factor, sequence_centred_unit, sequence_reciprocal_spread = (
        centred_sequences(sequence_embedding, sequence_layernorm_factor)
    )
    sequence_embedding_brief = sequence_scaled_by_factor.astype(jnp.bfloat16)
    content_sequences = jnp.dot(
        sequence_embedding_brief, content_projection, preferred_element_type=jnp.float32
    ).astype(jnp.bfloat16)
    value_per_head = content_sequences.reshape(
        device_sequences, device_residues, number_of_heads, head_channels
    )
    partial_value = jnp.einsum(
        "hij,sjhc->sihc", weight_panel, value_per_head, preferred_element_type=jnp.float32
    ).reshape(device_sequences, all_tokens, value_channels)
    partial_low = partial_value.astype(jnp.bfloat16)
    sigmoid_switch = jax.nn.sigmoid(
        jnp.dot(sequence_embedding_brief, switch_projection, preferred_element_type=jnp.float32)
    )
    pair_average = lax.psum_scatter(partial_low, "col", scatter_dimension=1, tiled=True).astype(
        jnp.float32
    )
    residual_change = jnp.dot(
        sigmoid_switch * pair_average, out_wide, precision=finest_accuracy
    ).astype(jnp.bfloat16)
    d_gated = jnp.dot(
        residual_change_cotangent.astype(jnp.float32), out_wide.T, precision=finest_accuracy
    )
    d_average_here = (sigmoid_switch * d_gated).astype(jnp.bfloat16)
    average_gradient = lax.all_gather(d_average_here, "col", axis=1, tiled=True)
    switch_preimage_sensitivity = d_gated * pair_average * sigmoid_switch * (1.0 - sigmoid_switch)
    gate_contribution = jnp.dot(
        switch_preimage_sensitivity, switch_single_form.T, precision=finest_accuracy
    )
    head_gradient = average_gradient.reshape(
        device_sequences, all_tokens, number_of_heads, head_channels
    )
    content_sensitivity = jnp.einsum(
        "hij,sihc->sjhc", weight_panel, head_gradient, preferred_element_type=jnp.float32
    )
    content_sensitivity = content_sensitivity.reshape(
        device_sequences, device_residues, value_channels
    ).astype(jnp.bfloat16)
    weight_part = jnp.einsum(
        "sihc,sjhc->hij", head_gradient, value_per_head, preferred_element_type=jnp.float32
    )
    d_weights = lax.psum_scatter(
        weight_part.astype(jnp.bfloat16), "bulk", scatter_dimension=1, tiled=True
    ).astype(jnp.float32)
    row_dot = lax.psum(jnp.sum(weights_low.astype(jnp.float32) * d_weights, axis=2), "col")
    d_logits = weights * (d_weights - row_dot[:, :, None])
    d_pair_low = jnp.einsum("hij,kh->ijk", d_logits, bias_wide, precision=finest_accuracy)
    coupling_sensitivity = layernorm_reverse_mode(
        d_pair_low, pair_hat, pair_inv, coupling_layernorm_factor
    ).astype(jnp.bfloat16)
    sequence_sensitivity_brief = (
        jnp.dot(content_sensitivity, content_projection.T, preferred_element_type=jnp.float32)
        + gate_contribution
    )
    sequence_embedding_sensitivity = layernorm_reverse_mode(
        sequence_sensitivity_brief,
        sequence_centred_unit,
        sequence_reciprocal_spread,
        sequence_layernorm_factor,
    ).astype(jnp.bfloat16)
    return (residual_change, sequence_embedding_sensitivity, coupling_sensitivity)


def solution(mesh):
    in_specs = (
        P("bulk", "col", None),
        P("bulk", "col", None),
        P(),
        P(),
        P(),
        P(),
        P(),
        P(),
        P("bulk", "col", None),
    )
    out_specs = (P("bulk", "col", None), P("bulk", "col", None), P("bulk", "col", None))
    return jax.shard_map(
        per_device, mesh=mesh, in_specs=in_specs, out_specs=out_specs, check_vma=False
    )
```

profile of v0, /device:TPU:0, one launch (start us, length us, event | category | flops | bytes accessed | tf_op | source)
XLA Modules:
  0.0 105.6 jit_solution(678878752773036502)
XLA Ops:
  7.2 0.0 copy-start
  7.2 0.0 copy-start.1
  7.2 0.0 reduce-scatter.5.cloned.1.call-start
  7.2 1.0 convert_reduce_fusion.1
  8.2 0.0 copy-done.1
  8.2 0.0 copy-start.4
  8.2 0.2 fusion.39
  8.4 0.0 copy-start.8
  8.5 0.5 copy-done.4
  9.0 0.1 copy-done.8
  9.1 0.2 convolution_convert_fusion.2
  9.4 0.0 copy-start.5
  9.4 0.2 reshape.60
  9.6 0.0 copy-done
  9.6 0.5 copy-done.5
  10.1 0.0 copy-start.6
  10.1 0.2 fusion.50
  10.3 0.6 copy-done.6
  10.9 0.3 multiply_convert_fusion
  11.2 11.5 %all_gather.7 = bf16[8,128,256]{2,1,0:T(8,128)(2,1)S(1)} all-gather(bf16[8,32,256]{2,1,0:T(8,128)(2,1)S(1)} %get-tuple-element.9), channel_id=1, replica_groups=mesh['col'=4,'bulk'=8] {'col'}, dimensions={1}, use_global_device_ids=true | all-gather | bytes 655360 | tf_op jit(solution)/shard_map/all_gather | solution.py:88
  22.7 0.3 copy.58
  23.0 0.3 fusion.6
  23.3 0.9 copy.64
  24.2 0.0 copy-start.2
  24.2 0.0 reduce-scatter.5.cloned.1.call-update
  24.2 0.0 reduce-scatter.3.cloned.1.call-start
  24.3 0.8 copy-done.2
  25.1 0.1 convert_reduce_fusion
  25.2 0.3 fusion.21
  25.5 0.0 copy-start.9
  25.5 0.0 copy-start.10
  25.5 0.6 copy-done.9
  26.2 0.0 copy-done.10
  26.2 0.4 fusion.65
  26.6 9.1 %psum.14 = f32[8,16]{0,1:T(8,128)S(1)} all-reduce(f32[8,16]{0,1:T(8,128)S(1)} %get-tuple-element.11), channel_id=1, replica_groups=mesh['col'=4,'bulk'=8] {'col'}, use_global_device_ids=true, to_apply=%region_5.0 | all-reduce | flops 128 | bytes 1024 | tf_op jit(solution)/shard_map/psum | solution.py:56
  35.7 19.7 %reduce-scatter.5.cloned.1.call-done = bf16[8,16,32]{2,0,1:T(8,128)(2,1)} async-done(((bf16[8,128,32]{2,0,1:T(8,128)(2,1)}), bf16[8,16,32]{2,0,1:T(8,128)(2,1)}) %reduce-scatter.5.cloned.1.call-update) | async-done | bytes 8208 | tf_op jit(solution)/shard_map/reduce_scatter | solution.py:105
  55.4 0.9 fusion.45
  56.3 14.2 %all_gather.6 = bf16[8,128,32]{2,0,1:T(8,128)(2,1)S(1)} all-gather(bf16[8,16,32]{2,0,1:T(8,128)(2,1)S(1)} %get-tuple-element.8), channel_id=1, replica_groups=mesh['col'=4,'bulk'=8] {'bulk'}, dimensions={1}, use_global_device_ids=true | all-gather | bytes 73728 | tf_op jit(solution)/shard_map/all_gather | solution.py:59
  70.5 0.4 fusion
  70.9 1.0 copy.57
  71.9 0.0 reduce-scatter.3.cloned.1.call-update
  71.9 0.3 fusion.1
  72.2 0.3 copy.61
  72.6 0.0 copy-start.7
  72.6 0.4 convert_element_type.78
  73.0 10.5 %psum.15 = f32[8,16]{0,1:T(8,128)S(1)} all-reduce(f32[8,16]{0,1:T(8,128)S(1)} %get-tuple-element.7), channel_id=1, replica_groups=mesh['col'=4,'bulk'=8] {'col'}, use_global_device_ids=true, to_apply=%region_11.0 | all-reduce | flops 128 | bytes 1024 | tf_op jit(solution)/shard_map/psum | solution.py:108
  83.4 0.0 copy-done.7
  83.4 0.7 fusion.62
  84.1 1.0 fusion.20
  85.1 10.4 %reduce-scatter.3.cloned.1.call-done = bf16[8,32,256]{2,1,0:T(8,128)(2,1)} async-done(((bf16[8,128,256]{2,1,0:T(8,128)(2,1)}), bf16[8,32,256]{2,1,0:T(8,128)(2,1)}) %reduce-scatter.3.cloned.1.call-update) | async-done | bytes 131088 | tf_op jit(solution)/shard_map/reduce_scatter | solution.py:78
  95.5 1.2 %fusion.24 = f32[8,32,64]{2,1,0:T(8,128)S(1)} fusion(f32[8,32,256]{2,1,0:T(8,128)S(1)} %get-tuple-element.10, f32[8,32,256]{2,1,0:T(8,128)S(1)} %fusion.50, bf16[8,32,256]{2,1,0:T(8,128)(2,1)} %reduce-scatter.3.cloned.1.call-done, bf16[64,256]{1,0:T(8,128)(2,1)S(1)} %copy-done.6), kind=kOutput, calls=%fused_computation.37 | convolution fusion | flops 50659328 | bytes 753664 | tf_op jit(solution)/shard_map/dot_general | solution.py:90
  96.7 0.3 fusion.63
  97.0 0.0 copy-start.3
  97.0 0.8 fusion.38
  97.9 0.1 copy-done.3
  97.9 0.9 convolution_convert_fusion.3
  (7 shorter events, 0.1 us)
Async XLA Ops:
  7.2 2.4 %copy-start = (bf16[8,32,64]{2,1,0:T(8,128)(2,1)S(1)}, bf16[8,32,64]{2,1,0:T(8,128)(2,1)}, u32[]{:S(2)}) copy-start(bf16[8,32,64]{2,1,0:T(8,128)(2,1)} %param.17) | copy-start | bytes 98308
  7.2 1.0 copy-start.1
  7.2 48.2 %reduce-scatter.5.cloned.1.call-start = ((), (), s32[]{:S(2)}) async-start(), calls=%async_computation.3 | async-start | bytes 294912 | tf_op jit(solution)/shard_map/reduce_scatter | solution.py:105
  8.2 0.8 copy-start.4
  8.4 0.7 copy-start.8
  9.4 0.8 copy-start.5
  10.1 0.8 copy-start.6
  24.2 0.9 copy-start.2
  24.2 71.3 %reduce-scatter.3.cloned.1.call-start = ((), (), s32[]{:S(2)}) async-start(), calls=%async_computation.2 | async-start | bytes 655360 | tf_op jit(solution)/shard_map/reduce_scatter | solution.py:78
  25.5 0.7 copy-start.9
  25.5 0.7 copy-start.10
  72.6 10.8 %copy-start.7 = (bf16[8,16,32]{2,0,1:T(8,128)(2,1)S(1)}, bf16[8,16,32]{2,0,1:T(8,128)(2,1)}, u32[]{:S(2)}) copy-start(bf16[8,16,32]{2,0,1:T(8,128)(2,1)} %reduce-scatter.5.cloned.1.call-done) | copy-start | bytes 24580
  97.0 0.9 copy-start.3
Sparse Core Ops, SparseCore 0:
  24.3 31.0 reduce-scatter.4
  72.1 23.4 reduce-scatter.2
where the time goes:
time: 106 us
  blocking collectives  45.3 us (43%)
  waiting for transfers between devices  30.1 us (28%)
  between operations  14.3 us (13%)
  local copies, waits for them, and re-layouts  6.44 us (6%)
  matrix products  5.12 us (5%)
  other arithmetic  4.33 us (4%)
    reduce_scatter x1, waiting for transfers between devices, per_device(): lax.psum_scatter(weight_part.astype(jnp.bfloat16), 'bulk', scatter_dimens...  19.7 us
    all_gather x1, blocking collectives, per_device(): weight_panel = lax.all_gather(weights_low, 'bulk', axis=1, tiled=True)  14.2 us
    all_gather x1, blocking collectives, per_device(): average_gradient = lax.all_gather(d_average_here, 'col', axis=1, tiled=True)  11.5 us
    psum x1, blocking collectives, per_device(): lax.psum(jnp.sum(weights_low.astype(jnp.float32) * d_weights, axis=2), 'c...  10.5 us
    reduce_scatter x1, waiting for transfers between devices, per_device(): lax.psum_scatter(partial_low, 'col', scatter_dimension=1, tiled=True)  10.4 us
    psum x1, blocking collectives, per_device(): totals = lax.psum(jnp.sum(exponent, axis=2), 'col')  9.09 us
    unnamed x22, local copies, waits for them, and re-layouts  3.31 us
  transfers between devices with their start and end apart: 2, of which 2 were waited for; matrix products, arithmetic and copies ran while one was open for 3% of the time, Pallas kernels for 0%

commit v1 on v0

--- a/solution.py
+++ b/solution.py
@@ -85,7 +85,7 @@
         residual_change_cotangent.astype(jnp.float32), out_wide.T, precision=finest_accuracy
     )
     d_average_here = (sigmoid_switch * d_gated).astype(jnp.bfloat16)
-    average_gradient = lax.all_gather(d_average_here, "col", axis=1, tiled=True)
+    average_gradient = jnp.concatenate(lax.all_gather(d_average_here, "col"), axis=1)
     switch_preimage_sensitivity = d_gated * pair_average * sigmoid_switch * (1.0 - sigmoid_switch)
     gate_contribution = jnp.dot(
         switch_preimage_sensitivity, switch_single_form.T, precision=finest_accuracy

time: 106 us -> 110 us (1.038)
  matrix products: 5.12 us -> 7.65 us
  waiting for transfers between devices: 30.1 us -> 31.6 us
    unnamed x22 -> x20, local copies, waits for them, and re-layouts: 3.31 us -> 0.06 us
    another operation x0 -> x2, local copies, waits for them, and re-layouts: none -> 2.4 us  [per_device(): average_gradient.reshape(device_sequences, all_tokens, number_of_heads, h...]
    reduce_scatter x1, waiting for transfers between devices: 19.7 us -> 21.2 us  [per_device(): lax.psum_scatter(weight_part.astype(jnp.bfloat16), 'bulk', scatter_dimens...]
where the time goes in v1:
time: 110 us; the launch traced here: 109 us
  blocking collectives  45.2 us (41%)
  waiting for transfers between devices  31.6 us (29%)
  between operations  14.4 us (13%)
  matrix products  7.65 us (7%)
  local copies, waits for them, and re-layouts  5.36 us (5%)
  other arithmetic  5.15 us (5%)
    reduce_scatter x1, waiting for transfers between devices, per_device(): lax.psum_scatter(weight_part.astype(jnp.bfloat16), 'bulk', scatter_dimens...  21.2 us
    all_gather x1, blocking collectives, per_device(): weight_panel = lax.all_gather(weights_low, 'bulk', axis=1, tiled=True)  14.2 us
    all_gather x1, blocking collectives, per_device(): lax.all_gather(d_average_here, 'col')  11.5 us
    psum x1, blocking collectives, per_device(): lax.psum(jnp.sum(weights_low.astype(jnp.float32) * d_weights, axis=2), 'c...  10.4 us
    reduce_scatter x1, waiting for transfers between devices, per_device(): lax.psum_scatter(partial_low, 'col', scatter_dimension=1, tiled=True)  10.4 us
    psum x1, blocking collectives, per_device(): totals = lax.psum(jnp.sum(exponent, axis=2), 'col')  9.09 us
    another operation x2, local copies, waits for them, and re-layouts, per_device(): average_gradient.reshape(device_sequences, all_tokens, number_of_heads, h...  2.4 us
  transfers between devices with their start and end apart: 2, of which 2 were waited for; matrix products, arithmetic and copies ran while one was open for 3% of the time, Pallas kernels for 0%

profile of v1, /device:TPU:0, one launch (start us, length us, event | category | flops | bytes accessed | tf_op | source)
XLA Modules:
  0.0 109.4 jit_solution(8291395642825709479)
XLA Ops:
  7.2 0.0 copy-start
  7.2 0.0 reduce-scatter.5.cloned.1.call-start
  7.2 0.9 convert_reduce_fusion.1
  8.2 1.0 fusion.38
  9.2 0.0 copy-done
  9.2 0.9 fusion.49
  10.2 1.1 %multiply_convert_fusion = (bf16[8,32,256]{2,1,0:T(8,128)(2,1)S(1)}, f32[8,32,256]{2,1,0:T(8,128)S(1)}) fusion(f32[8,32,256]{2,1,0:T(8,128)S(1)} %fusion.49, bf16[64,256]{1,0:T(8,128)(2,1)} %param.14, bf16[8,32,64]{2,1,0:T(8,128)(2,1)} %param.9, f32[64]{0:T(128)} %param.11, f32[8,32]{1,0:T(8,128)S(1)} %add_rsqrt_fusion.1, ...), kind=kOutput, calls=%fused_computation.39 | convolution fusion | flops 8798208 | bytes 723200 | tf_op jit(solution)/shard_map/dot_general | solution.py:76
  11.3 11.5 %all-gather = bf16[32,32,256]{2,1,0:T(8,128)(2,1)S(1)} all-gather(bf16[8,32,256]{2,1,0:T(8,128)(2,1)S(1)} %get-tuple-element.9), channel_id=2, replica_groups=mesh['col'=4,'bulk'=8] {'col'}, dimensions={0}, use_global_device_ids=true | all-gather | bytes 655360 | tf_op jit(solution)/shard_map/all_gather | solution.py:88
  22.9 0.0 copy-start.1
  22.9 0.0 copy-start.3
  22.9 0.0 copy-start.7
  22.9 0.9 reshape_reshape.3
  23.8 0.0 copy-start.2
  23.8 1.5 %copy.59 = bf16[8,128,8,32]{1,3,0,2:T(8,128)(2,1)S(1)} copy(bf16[8,128,8,32]{3,2,1,0:T(8,128)(2,1)S(1)} %reshape_reshape.3) | data formatting | bytes 1048576 | tf_op jit(solution)/shard_map/reshape;reshape | solution.py:93
  25.3 0.0 copy-done.1
  25.3 0.0 copy-done.3
  25.3 0.0 copy-done.7
  25.4 0.0 copy-start.8
  25.4 0.0 copy-start.9
  25.4 0.3 convolution_convert_fusion.2
  25.6 0.2 reshape.60
  25.9 0.3 fusion.6
  26.2 0.9 copy.65
  27.1 0.0 reduce-scatter.5.cloned.1.call-update
  27.1 0.0 reduce-scatter.3.cloned.1.call-start
  27.2 0.0 copy-done.2
  27.2 0.1 convert_reduce_fusion
  27.3 0.3 fusion.20
  27.6 0.0 copy-done.8
  27.6 0.0 copy-done.9
  27.6 0.4 fusion.64
  28.1 9.1 %psum.14 = f32[8,16]{0,1:T(8,128)S(1)} all-reduce(f32[8,16]{0,1:T(8,128)S(1)} %get-tuple-element.11), channel_id=1, replica_groups=mesh['col'=4,'bulk'=8] {'col'}, use_global_device_ids=true, to_apply=%region_5.0 | all-reduce | flops 128 | bytes 1024 | tf_op jit(solution)/shard_map/psum | solution.py:56
  37.2 21.2 %reduce-scatter.5.cloned.1.call-done = bf16[8,16,32]{2,0,1:T(8,128)(2,1)} async-done(((bf16[8,128,32]{2,0,1:T(8,128)(2,1)}), bf16[8,16,32]{2,0,1:T(8,128)(2,1)}) %reduce-scatter.5.cloned.1.call-update) | async-done | bytes 8208 | tf_op jit(solution)/shard_map/reduce_scatter | solution.py:105
  58.4 0.9 fusion.44
  59.3 14.2 %all_gather.9 = bf16[8,128,32]{2,0,1:T(8,128)(2,1)S(1)} all-gather(bf16[8,16,32]{2,0,1:T(8,128)(2,1)S(1)} %get-tuple-element.8), channel_id=1, replica_groups=mesh['col'=4,'bulk'=8] {'bulk'}, dimensions={1}, use_global_device_ids=true | all-gather | bytes 73728 | tf_op jit(solution)/shard_map/all_gather | solution.py:59
  73.5 0.4 fusion
  73.9 0.0 copy-start.6
  73.9 1.0 copy.57
  74.9 0.0 reduce-scatter.3.cloned.1.call-update
  74.9 0.0 copy-start.5
  74.9 0.3 fusion.1
  75.2 0.3 copy.61
  75.6 0.0 copy-start.4
  75.6 0.4 convert_element_type.78
  76.0 10.4 %psum.15 = f32[8,16]{0,1:T(8,128)S(1)} all-reduce(f32[8,16]{0,1:T(8,128)S(1)} %get-tuple-element.7), channel_id=1, replica_groups=mesh['col'=4,'bulk'=8] {'col'}, use_global_device_ids=true, to_apply=%region_11.0 | all-reduce | flops 128 | bytes 1024 | tf_op jit(solution)/shard_map/psum | solution.py:108
  86.4 0.0 copy-done.6
  86.4 0.7 fusion.61
  87.1 1.0 fusion.19
  88.1 10.4 %reduce-scatter.3.cloned.1.call-done = bf16[8,32,256]{2,1,0:T(8,128)(2,1)} async-done(((bf16[8,128,256]{2,1,0:T(8,128)(2,1)}), bf16[8,32,256]{2,1,0:T(8,128)(2,1)}) %reduce-scatter.3.cloned.1.call-update) | async-done | bytes 131088 | tf_op jit(solution)/shard_map/reduce_scatter | solution.py:78
  98.4 0.0 copy-done.5
  98.4 1.2 %fusion.23 = f32[8,32,64]{2,1,0:T(8,128)S(1)} fusion(f32[8,32,256]{2,1,0:T(8,128)S(1)} %get-tuple-element.10, f32[8,32,256]{2,1,0:T(8,128)S(1)} %fusion.49, bf16[8,32,256]{2,1,0:T(8,128)(2,1)} %reduce-scatter.3.cloned.1.call-done, bf16[64,256]{1,0:T(8,128)(2,1)S(1)} %copy-done.5), kind=kOutput, calls=%fused_computation.37 | convolution fusion | flops 50659328 | bytes 753664 | tf_op jit(solution)/shard_map/dot_general | solution.py:90
  99.6 0.3 fusion.62
  99.9 0.8 fusion.37
  100.8 0.0 copy-done.4
  100.8 1.8 %convolution_convert_fusion.3 = bf16[8,32,64]{2,1,0:T(8,128)(2,1)} fusion(f32[8,32,256]{2,1,0:T(8,128)S(1)} %get-tuple-element.10, bf16[8,32,256]{2,1,0:T(8,128)(2,1)} %reduce-scatter.3.cloned.1.call-done, bf16[256,64]{0,1:T(8,128)(2,1)S(1)} %copy-done.4), kind=kOutput, calls=%fused_computation.14 | convolution fusion | flops 50479104 | bytes 458752 | tf_op jit(solution)/shard_map/dot_general | solution.py:81
  (8 shorter events, 0.1 us)
Async XLA Ops:
  7.2 2.1 %copy-start = (bf16[8,32,64]{2,1,0:T(8,128)(2,1)S(1)}, bf16[8,32,64]{2,1,0:T(8,128)(2,1)}, u32[]{:S(2)}) copy-start(bf16[8,32,64]{2,1,0:T(8,128)(2,1)} %param.17) | copy-start | bytes 98308
  7.2 51.2 %reduce-scatter.5.cloned.1.call-start = ((), (), s32[]{:S(2)}) async-start(), calls=%async_computation.3 | async-start | bytes 294912 | tf_op jit(solution)/shard_map/reduce_scatter | solution.py:105
  22.9 2.5 %copy-start.1 = (bf16[8,32,64]{2,1,0:T(8,128)(2,1)S(1)}, bf16[8,32,64]{2,1,0:T(8,128)(2,1)}, u32[]{:S(2)}) copy-start(bf16[8,32,64]{2,1,0:T(8,128)(2,1)} %param.9) | copy-start | bytes 98308
  22.9 2.5 %copy-start.3 = (bf16[64,256]{1,0:T(8,128)(2,1)S(1)}, bf16[64,256]{1,0:T(8,128)(2,1)}, u32[]{:S(2)}) copy-start(bf16[64,256]{1,0:T(8,128)(2,1)} %param.13) | copy-start | bytes 98308
  22.9 2.5 %copy-start.7 = (f32[64]{0:T(128)S(1)}, f32[64]{0:T(128)}, u32[]{:S(2)}) copy-start(f32[64]{0:T(128)} %param.11) | copy-start | bytes 772
  23.8 3.4 %copy-start.2 = (bf16[16,32,128]{2,1,0:T(8,128)(2,1)S(1)}, bf16[16,32,128]{2,1,0:T(8,128)(2,1)}, u32[]{:S(2)}) copy-start(bf16[16,32,128]{2,1,0:T(8,128)(2,1)} %param.10) | copy-start | bytes 393220
  25.4 2.3 %copy-start.8 = (bf16[128,8]{0,1:T(8,128)(2,1)S(1)}, bf16[128,8]{0,1:T(8,128)(2,1)}, u32[]{:S(2)}) copy-start(bf16[128,8]{0,1:T(8,128)(2,1)} %param.15) | copy-start | bytes 6148
  25.4 2.3 %copy-start.9 = (f32[128]{0:T(128)S(1)}, f32[128]{0:T(128)}, u32[]{:S(2)}) copy-start(f32[128]{0:T(128)} %param.12) | copy-start | bytes 1540
  27.1 71.3 %reduce-scatter.3.cloned.1.call-start = ((), (), s32[]{:S(2)}) async-start(), calls=%async_computation.2 | async-start | bytes 655360 | tf_op jit(solution)/shard_map/reduce_scatter | solution.py:78
  73.9 12.5 %copy-start.6 = (bf16[8,16,32]{2,0,1:T(8,128)(2,1)S(1)}, bf16[8,16,32]{2,0,1:T(8,128)(2,1)}, u32[]{:S(2)}) copy-start(bf16[8,16,32]{2,0,1:T(8,128)(2,1)} %reduce-scatter.5.cloned.1.call-done) | copy-start | bytes 24580
  74.9 23.5 %copy-start.5 = (bf16[64,256]{1,0:T(8,128)(2,1)S(1)}, bf16[64,256]{1,0:T(8,128)(2,1)}, u32[]{:S(2)}) copy-start(bf16[64,256]{1,0:T(8,128)(2,1)} %param.14) | copy-start | bytes 98308
  75.6 25.2 %copy-start.4 = (bf16[256,64]{0,1:T(8,128)(2,1)S(1)}, bf16[256,64]{0,1:T(8,128)(2,1)}, u32[]{:S(2)}) copy-start(bf16[256,64]{0,1:T(8,128)(2,1)} %param.16) | copy-start | bytes 98308
Sparse Core Ops, SparseCore 0:
  27.2 31.0 reduce-scatter.4
  75.0 23.3 reduce-scatter.2
